TPU v7x, 256 devices: a whole 4x4x8 slice. The times are simulated.
256 devices in a mesh: seq: 32 (over x, y, core), pipe: 8 (over z).
Axes of the slice: x: 4, y: 4, z: 8, core: 2. Of those that a mesh axis runs over, the one named last changes fastest.
Arguments:
- section_inputs: bfloat16 [8, 4096, 1536], P('pipe', 'seq'), may hold values from -6 to 6
- cotangent: bfloat16 [4096, 1536], P('seq'), may hold values from -6 to 6
- gain: float32 [8, 1536], P('pipe'), may hold values from 0.25 to 1.75
- w_gate: bfloat16 [8, 1536, 1536], P('pipe'), may hold values from -0.15625 to 0.15625
- w_out: bfloat16 [8, 1536, 1536], P('pipe'), may hold values from -0.15625 to 0.15625
- mix_first: bfloat16 [8, 64, 64, 64], P('pipe', 'seq'), may hold values from -0.75 to 0.75
- mix_second: bfloat16 [8, 64, 64, 64], P('pipe', 'seq'), may hold values from -0.75 to 0.75
Outputs:
- grad_inputs: bfloat16 [8, 4096, 1536], P('pipe', 'seq')
- grad_first: float32 [8, 64, 64, 64], P('pipe', 'seq')
- grad_second: float32 [8, 64, 64, 64], P('pipe', 'seq')
All inputs are finite; a program needn't handle non-finite values.
Results may differ from a plain program's by a relative error of at most 0.025.
Values may be sent and summed in bfloat16 or wider, within the bound.
A program may use at most 64 MiB of HBM per device.

v0:
```python
import functools

import jax
import jax.numpy as jnp
from jax import lax
from jax.experimental import pallas as pl
from jax.experimental.pallas import tpu as pltpu
from jax.sharding import PartitionSpec as P

MESH = pl.DeviceIdType.MESH
F32 = jnp.float32
BF16 = jnp.bfloat16
LANES = 128
CUTS = 4
CHUNK = LANES * CUTS
ROWS_TO = 4
PIECE = ROWS_TO * CUTS


def iota(shape, axis):
    return lax.broadcasted_iota(jnp.int32, shape, axis)


def dot(a, b, da=1, db=0):
    return lax.dot_general(a, b, (((da,), (db,)), ((), ())), preferred_element_type=F32)


def as_bf16(mask):
    return jnp.where(mask, 1.0, 0.0).astype(BF16)


SCRATCH = (
    "x", "gain", "wg", "wo", "m1", "m2", "xnext", "xw", "inv", "shift",
    "nrm", "nst", "dfwd", "efwd", "dbwd", "ebwd", "pick1", "pick2", "fsend", "frecv",
    "bsend", "brecv", "moved", "mf", "gf", "dh", "dmix", "dgate", "gb", "anat",
    "abuf", "csend", "crecv", "res", "r1", "r2", "lsem", "osem", "xs_sem", "xr_sem",
    "fs_sem", "fr_sem", "bs_sem", "br_sem", "zs_sem", "zr_sem", "cs_sem", "cr_sem", "ws_sem", "wz_sem", "wxs_sem", "wxr_sem", "wys_sem", "wyr_sem", "wds_sem", "wdr_sem", "wcs_sem", "wc_sem", "ps_sem", "pr_sem", "rs_sem", "rr_sem",
)


class Refs:
    pass


def kernel(
    n_seq, n_pipe, x_hbm, cot_hbm, gain_hbm, wg_hbm, wo_hbm, m1_hbm, m2_hbm, out_hbm, g1_hbm, g2_hbm, *scratch
):
    r = Refs()
    for name, ref in zip(SCRATCH, scratch, strict=True):
        setattr(r, name, ref)
    me = lax.axis_index("seq")
    plane = lax.axis_index("pipe")
    _, rows, width = r.x.shape
    block = rows // 2
    chunks = width // CHUNK
    span = n_seq * PIECE
    whole = slice(0, chunks * LANES)
    tiles = [(f, c, (f * CUTS + c) * LANES) for f in range(chunks) for c in range(CUTS)]

    first = plane == 7
    final = plane == 0
    double = (plane == 4) | final
    supplier = (plane == 3) | (plane == 1)
    worker = jnp.logical_not(supplier)
    single = worker & jnp.logical_not(double)
    mate = jnp.where(plane >= 3, 7 - plane, 1 - plane)
    own = jnp.where(final, 1, 0)
    guest = 1 - own
    before = lax.rem(plane + n_pipe - 1, n_pipe)
    following = jnp.where(plane == 4, 2, jnp.where(plane == 2, 0, before))
    reader = jnp.where(plane == 2, 0, before)
    far = 8 if n_seq == 32 else 4
    bit_x, bit_y, bit_c = (me // far) % 2, (me // 2) % 2, me % 2
    x_mate = me + far - 2 * far * bit_x
    y_mate = me + 2 - 4 * bit_y
    core_mate = me + 1 - 2 * bit_c
    slab = width // 16

    def seq_at(device):
        return {"seq": device}

    def pipe_at(device):
        return {"pipe": device}

    def remote(src, dst, send_sem, recv_sem, device):
        return pltpu.make_async_remote_copy(
            src_ref=src,
            dst_ref=dst,
            send_sem=send_sem,
            recv_sem=recv_sem,
            device_id=device,
            device_id_type=MESH,
        )

    def landed(ref, sem):
        pltpu.make_async_copy(ref, ref, sem).wait()

    loads = [
        pltpu.make_async_copy(src, dst, r.lsem.at[i])
        for i, (src, dst) in enumerate(
            (
                (x_hbm, r.x.at[own]),
                (m1_hbm, r.m1.at[own]),
                (m2_hbm, r.m2.at[own]),
                (gain_hbm, r.gain.at[own]),
                (wg_hbm, r.wg.at[own]),
                (wo_hbm, r.wo.at[own]),
            )
        )
    ]

    @pl.when(worker)
    def _():
        for copy in loads:
            copy.start()

    def cot_copy(f):
        return pltpu.make_async_copy(
            cot_hbm.at[:, f * CHUNK : (f + 1) * CHUNK], r.abuf.at[0, f], r.zr_sem.at[f]
        )

    @pl.when(first)
    def _():
        for f in range(chunks):
            cot_copy(f).start()

    barrier = pltpu.get_barrier_semaphore()

    @pl.loop(1, n_seq)
    def _(i):
        pl.semaphore_signal(
            barrier, inc=1, device_id=seq_at(lax.rem(me + i, n_seq)), device_id_type=MESH
        )

    @pl.loop(1, n_pipe)
    def _(i):
        pl.semaphore_signal(
            barrier, inc=1, device_id=pipe_at(lax.rem(plane + i, n_pipe)), device_id_type=MESH
        )

    def exchange(send, recv, send_sem, recv_sem, lanes):
        mine = pl.ds(pl.multiple_of(me * PIECE, PIECE), PIECE)
        pltpu.make_async_copy(send.at[mine, lanes], recv.at[mine, lanes], recv_sem).start()

        @pl.loop(1, n_seq)
        def _(i):
            to = lax.rem(me + i, n_seq)
            theirs = pl.ds(pl.multiple_of(to * PIECE, PIECE), PIECE)
            remote(send.at[theirs, lanes], recv.at[mine, lanes], send_sem, recv_sem, seq_at(to)).start()

    def sent(send, send_sem, lanes):
        landed(send.at[: span - PIECE, lanes], send_sem)

    spot = iota((span, rows), 0)
    col = iota((span, rows), 1)
    dest = spot // PIECE
    quad = spot % ROWS_TO
    cut_of = (spot // ROWS_TO) % CUTS
    spot_t = iota((rows, span), 1)
    row_t = iota((rows, span), 0)
    dest_t = spot_t // PIECE
    quad_t = spot_t % ROWS_TO
    cut_of_t = (spot_t // ROWS_TO) % CUTS

    def sel1():
        return as_bf16(col == (quad % 2) * block + dest * 2 + quad // 2)

    def sel2():
        return as_bf16(col == (quad // 2) * block + dest * 2 + quad % 2)

    def sel1_t():
        return as_bf16(row_t == (quad_t % 2) * block + dest_t * 2 + quad_t // 2)

    def sel2_t():
        return as_bf16(row_t == (quad_t // 2) * block + dest_t * 2 + quad_t % 2)

    def diagonal(blocks):
        spread = as_bf16(iota((block, rows), 0) == iota((block, rows), 1) % block)
        wide = dot(blocks, spread)
        same = iota((rows, rows), 0) // block == iota((rows, rows), 1) // block
        return jnp.where(same, wide, 0.0).astype(BF16)

    def put_tall(ref, value):
        for c in range(CUTS):
            ref[:, c * rows : (c + 1) * rows] = jnp.where(cut_of == c, value, 0.0).astype(BF16)

    def put_flat(ref, value):
        for c in range(CUTS):
            ref[c * rows : (c + 1) * rows, :] = jnp.where(cut_of_t == c, value, 0.0).astype(BF16)

    def factors(at):
        d1 = diagonal(r.m1[at])
        d2 = diagonal(r.m2[at])
        put_tall(r.dfwd, dot(sel1(), d1))
        put_tall(r.dbwd.at[at], dot(sel2(), d2, 1, 1))
        put_flat(r.efwd, dot(d2, sel2_t()))
        put_flat(r.ebwd.at[at], dot(d1, sel1_t(), 0, 0))

    def norm(at):
        total = jnp.zeros((rows, LANES), F32)
        for _, _, t in tiles:
            v = r.x[at, :, t : t + LANES].astype(F32)
            total += v * v
        scale = lax.rsqrt(jnp.sum(total, axis=-1, keepdims=True) / width + 1e-06)
        scale = jnp.broadcast_to(scale, (rows, LANES))
        r.inv[at] = scale
        for f, c, t in tiles:
            v = r.x[at, :, t : t + LANES].astype(F32) * scale * r.gain[at, :, t : t + LANES]
            v = v.astype(BF16)
            r.nrm[:, t : t + LANES] = v
            r.nst[at, c * rows : (c + 1) * rows, f * LANES : (f + 1) * LANES] = v
        r.fsend[at] = dot(r.dfwd[...], r.nst[at]).astype(BF16)

    def forward(at):
        exchange(r.fsend.at[at], r.frecv.at[at], r.fs_sem.at[at], r.fr_sem.at[at], whole)

    def gate(at):
        for f in range(chunks):
            cols = slice(f * CHUNK, (f + 1) * CHUNK)
            pre = dot(r.nrm[...], r.wg[at, :, cols])
            s = jax.nn.sigmoid(pre)
            r.mf[at, :, cols] = pre * s
            r.gf[at, :, cols] = s * (1.0 + pre * (1.0 - s))

    def mixer(at):
        landed(r.frecv.at[at], r.fr_sem.at[at])
        mixed = dot(r.efwd[...], r.frecv[at])
        natural = dot(r.pick2[...], r.frecv[at]).astype(BF16)
        for f, c, t in tiles:
            part = (slice(c * rows, (c + 1) * rows), slice(f * LANES, (f + 1) * LANES))
            r.gf[at, :, t : t + LANES] = r.gf[at, :, t : t + LANES] * mixed[part]
            r.moved[at, :, t : t + LANES] = natural[part]

    @pl.when(worker)
    def _():
        loads[1].wait()
        loads[2].wait()
        put_flat(r.pick1, sel1_t().astype(F32))
        put_flat(r.pick2, sel2_t().astype(F32))
        factors(own)
        loads[0].wait()
        loads[3].wait()
        norm(own)

    pl.semaphore_wait(barrier, n_seq + n_pipe - 2)

    x_copy = remote(x_hbm, r.xnext, r.xs_sem, r.xr_sem, pipe_at(reader))
    x_sender = single | (plane == 3)
    there = jnp.where(plane == 1, 0, 1)

    def slab_at(flip_x, flip_y, j):
        unit = 4 * (1 - bit_x if flip_x else bit_x) + 2 * (1 - bit_y if flip_y else bit_y) + bit_c
        return pl.ds(pl.multiple_of((2 * unit + j) * slab, slab), slab)

    def supply():
        given = []
        for i, (src, dst) in enumerate(((wg_hbm, r.wg), (wo_hbm, r.wo))):
            for j in range(2):
                at = slab_at(0, 0, j)
                given.append(
                    remote(
                        src.at[at],
                        dst.at[there, at],
                        r.ws_sem.at[i, j],
                        r.wz_sem.at[i, j],
                        pipe_at(mate),
                    )
                )
        small = [
            remote(src, dst.at[there], r.ps_sem.at[k], r.pr_sem.at[k], pipe_at(mate))
            for k, (src, dst) in enumerate(
                ((x_hbm, r.x), (m1_hbm, r.m1), (m2_hbm, r.m2), (gain_hbm, r.gain))
            )
        ]
        return given + small[1:] + small[:1]

    @pl.when(x_sender)
    def _():
        x_copy.start()

    @pl.when(supplier)
    def _():
        for copy in supply():
            copy.start()

    def weight(i):
        return r.wo if i else r.wg

    def piece(i, j, flip_x=0, flip_y=0):
        return weight(i).at[guest, slab_at(flip_x, flip_y, j)]

    def pass_own(i, j):
        ref = piece(i, j)
        return (
            remote(ref, ref, r.wxs_sem.at[i, j], r.wxr_sem.at[i, j], seq_at(x_mate)),
            remote(ref, ref, r.wys_sem.at[i, j], r.wyr_sem.at[i, j], seq_at(y_mate)),
            remote(ref, ref, r.wcs_sem.at[0, i, j], r.wc_sem.at[i], seq_at(core_mate)),
        )

    def pass_core(i, j, flip_x, flip_y):
        ref = piece(i, j, flip_x, flip_y)
        send_sem = r.wcs_sem.at[flip_x + 2 * flip_y, i, j]
        return remote(ref, ref, send_sem, r.wc_sem.at[i], seq_at(core_mate))

    def pass_corner(i, j, flip_x, flip_y):
        ref = piece(i, j, flip_x, flip_y)
        to = y_mate if flip_x else x_mate
        return remote(ref, ref, r.wds_sem.at[i, j], r.wdr_sem.at[i, j], seq_at(to))

    def collect_own(i, j):
        landed(piece(i, j), r.wz_sem.at[i, j])
        for copy in pass_own(i, j):
            copy.start()

    def collect_sides(i, j):
        landed(piece(i, j, 1, 0), r.wxr_sem.at[i, j])

        @pl.when(bit_c == 0)
        def _():
            pass_corner(i, j, 1, 0).start()

        pass_core(i, j, 1, 0).start()
        landed(piece(i, j, 0, 1), r.wyr_sem.at[i, j])

        @pl.when(bit_c == 1)
        def _():
            pass_corner(i, j, 0, 1).start()

        pass_core(i, j, 0, 1).start()

    def collect_corner(i, j):
        landed(piece(i, j, 1, 1), r.wdr_sem.at[i, j])
        pass_core(i, j, 1, 1).start()

    def collect_rest(i):
        landed(weight(i).at[guest, : 8 * slab], r.wc_sem.at[i])

    def finish_guest():
        for j in range(2):
            collect_corner(1, j)
        collect_rest(1)
        mixer(guest)

    @pl.when(worker)
    def _():
        forward(own)
        loads[4].wait()
        gate(own)
        loads[5].wait()

    @pl.when(worker & jnp.logical_not(first))
    def _():
        mixer(own)

    def hidden_of(ref, at):
        for f in range(chunks):
            cols = slice(f * CHUNK, (f + 1) * CHUNK)
            r.xw[at, :, cols] = dot(ref[...], r.wo[at, cols, :], 1, 1)

    @pl.when(worker & jnp.logical_not(first))
    def _():
        x_copy.wait_recv()

    @pl.when(worker & jnp.logical_not(first) & jnp.logical_not(final))
    def _():
        hidden_of(r.xnext, 0)

    @pl.when(double)
    def _():
        collect_own(0, 0)
        collect_own(0, 1)
        collect_sides(0, 0)
        collect_own(1, 0)
        collect_sides(0, 1)
        collect_own(1, 1)
        collect_corner(0, 0)
        collect_corner(0, 1)
        collect_sides(1, 0)
        for k, ref in ((1, r.m1), (2, r.m2), (3, r.gain)):
            landed(ref.at[guest], r.pr_sem.at[k])
        factors(guest)
        collect_sides(1, 1)
        landed(r.x.at[guest], r.pr_sem.at[0])
        norm(guest)
        forward(guest)
        collect_rest(0)
        gate(guest)

    @pl.when(double)
    def _():
        finish_guest()
        hidden_of(r.x.at[0], 1)

    @pl.when(final)
    def _():
        hidden_of(r.xnext, 0)

    @pl.when(first)
    def _():
        r.shift[...] = jnp.zeros(r.shift.shape, F32)
        r.xw[0] = jnp.zeros((rows, width), F32)
        r.xnext[...] = jnp.zeros(r.xnext.shape, BF16)

    eye = iota((rows, rows), 0) == iota((rows, rows), 1)
    c_copy = remote(r.csend, r.crecv, r.cs_sem, r.cr_sem, pipe_at(following))

    def hand(slot, f):
        return remote(
            r.abuf.at[slot + 1, f],
            r.abuf.at[0, f],
            r.zs_sem.at[f],
            r.zr_sem.at[f],
            pipe_at(following),
        )

    def partial(slot, k):
        deep = slice(k * CHUNK, (k + 1) * CHUNK)
        for f in range(chunks):
            cols = slice(f * CHUNK, (f + 1) * CHUNK)
            part = dot(r.abuf[slot, k], r.wo[slot, cols, deep], 1, 1)
            r.dh[:, cols] = part if k == 0 else r.dh[:, cols] + part

    def results(slot):
        inv = r.inv.at[slot]
        natural = dot(r.pick1[...], r.brecv[slot]).astype(BF16)
        sums = jnp.zeros((rows, rows), F32)
        for c in range(CUTS):
            part = slice(c * rows, (c + 1) * rows)
            sums += dot(natural[part, :], r.nst[slot, part, :], 1, 1)
        for a in range(2):
            r.r1[slot, a] = sums[a * block : (a + 1) * block, a * block : (a + 1) * block]

    def outgoing(slot):
        for _, _, t in tiles:
            cols = slice(t, t + LANES)
            r.res[slot, :, cols] = (
                r.anat[:, cols] - r.shift[...] * r.x[slot, :, cols].astype(F32)
            ).astype(BF16)

    def stores(slot):
        return [
            pltpu.make_async_copy(src.at[slot], dst, r.osem.at[k])
            for k, (src, dst) in enumerate(((r.res, out_hbm), (r.r1, g1_hbm), (r.r2, g2_hbm)))
        ]

    def returns(slot, kinds=range(3)):
        pairs = ((r.res, out_hbm), (r.r1, g1_hbm), (r.r2, g2_hbm))
        return [
            remote(
                pairs[k][0].at[slot], pairs[k][1], r.rs_sem.at[k], r.rr_sem.at[k], pipe_at(mate)
            )
            for k in kinds
        ]

    def chain(slot):
        if slot == 0:
            for k in range(chunks):
                cot_copy(k).wait()
                if k < chunks - 1:
                    partial(0, k)

            @pl.when(jnp.logical_not(first))
            def _():
                c_copy.wait_recv()
                spread = jnp.where(eye, jnp.broadcast_to(r.crecv[0:1, :], (rows, rows)), 0.0)
                r.shift[...] = jnp.broadcast_to(
                    jnp.sum(spread, axis=1, keepdims=True), r.shift.shape
                )

        k = chunks - 1
        deep = slice(k * CHUNK, (k + 1) * CHUNK)
        for f in range(chunks):
            cols = slice(f * CHUNK, (f + 1) * CHUNK)
            hidden = r.dh[:, cols] + dot(r.abuf[slot, k], r.wo[slot, cols, deep], 1, 1)
            hidden = hidden - r.shift[:, :1] * r.xw[slot, :, cols]
            r.dh[:, cols] = hidden
            mix = (hidden * r.mf[slot, :, cols]).astype(BF16)
            r.dmix[:, cols] = mix
            stack = jnp.concatenate(
                [mix[:, c * LANES : (c + 1) * LANES] for c in range(CUTS)], axis=0
            )
            lanes = slice(f * LANES, (f + 1) * LANES)
            r.bsend[slot, :, lanes] = dot(r.dbwd[slot], stack).astype(BF16)
            exchange(
                r.bsend.at[slot],
                r.brecv.at[slot],
                r.bs_sem.at[slot, f],
                r.br_sem.at[slot, f],
                lanes,
            )
        if slot == 0:

            @pl.when(first)
            def _():
                mixer(0)

        r.dgate[...] = (r.dh[...] * r.gf[slot]).astype(BF16)
        for f in range(chunks):
            cols = slice(f * CHUNK, (f + 1) * CHUNK)
            r.gb[:, cols] = dot(r.dgate[...], r.wg[slot, cols, :], 1, 1)
        g2 = dot(r.dmix[...], r.moved[slot], 1, 1)
        for a in range(2):
            r.r2[slot, a] = g2[a * block : (a + 1) * block, a * block : (a + 1) * block]
        if slot == 1:
            results(0)

            @pl.when(final)
            def _():
                for copy in returns(0, (1, 2)):
                    copy.start()

        sending = single if slot == 0 else jnp.logical_not(final)
        inv = r.inv.at[slot]
        total = jnp.zeros((rows, LANES), F32)
        for f in range(chunks):
            lanes = slice(f * LANES, (f + 1) * LANES)
            landed(r.brecv.at[slot, :, lanes], r.br_sem.at[slot, f])
            back = dot(r.ebwd[slot], r.brecv[slot, :, lanes])
            for c in range(CUTS):
                t = f * CHUNK + c * LANES
                cols = slice(t, t + LANES)
                delta = r.gain[slot, :, cols] * (back[c * rows : (c + 1) * rows, :] + r.gb[:, cols])
                unit = r.x[slot, :, cols].astype(F32) * inv[...]
                total += delta * unit
                here = slice(c * LANES, (c + 1) * LANES)
                prior = r.xnext[:, cols] if slot == 0 else r.x[0, :, cols]
                incoming = r.abuf[slot, f, :, here].astype(F32) - r.shift[...] * prior.astype(F32)
                value = incoming + inv[...] * delta
                r.anat[:, cols] = value
                r.abuf[slot + 1, f, :, here] = value.astype(BF16)
            if f < chunks - 1:

                @pl.when(sending)
                def _():
                    hand(slot, f).start()

                if slot == 0:

                    @pl.when(double)
                    def _():
                        partial(1, f)

        mean = jnp.sum(total, axis=-1, keepdims=True) / width
        fix = jnp.broadcast_to(mean, (rows, LANES)) * inv[...] * inv[...]

        @pl.when(sending)
        def _():
            line = jnp.sum(jnp.where(eye, fix[:, :1], 0.0), axis=0, keepdims=True)
            r.csend[...] = jnp.broadcast_to(line, r.csend.shape)
            c_copy.start()
            hand(slot, chunks - 1).start()

        r.shift[...] = fix
        outgoing(slot)
        if slot == 0:

            @pl.when(final)
            def _():
                returns(0, (0,))[0].start()

    @pl.when(worker)
    def _():
        chain(0)

    @pl.when(single)
    def _():
        results(0)

    @pl.when(double)
    def _():
        chain(1)
        results(1)

    @pl.when(double & jnp.logical_not(final))
    def _():
        c_copy.wait_send()
        for f in range(chunks):
            hand(1, f).wait_send()
        for copy in returns(1):
            copy.start()

    @pl.when(worker)
    def _():
        for copy in stores(own):
            copy.start()
        sent(r.fsend.at[own], r.fs_sem.at[own], whole)
        for f in range(chunks):
            sent(r.bsend.at[0], r.bs_sem.at[0, f], slice(f * LANES, (f + 1) * LANES))

    @pl.when(double)
    def _():
        sent(r.fsend.at[guest], r.fs_sem.at[guest], whole)
        for f in range(chunks):
            sent(r.bsend.at[1], r.bs_sem.at[1, f], slice(f * LANES, (f + 1) * LANES))
        for i in range(2):
            for j in range(2):
                for copy in pass_own(i, j):
                    copy.wait_send()
                pass_core(i, j, 1, 0).wait_send()
                pass_core(i, j, 0, 1).wait_send()
                pass_core(i, j, 1, 1).wait_send()
                pass_corner(i, j, 1, 0).wait_send()
        for copy in returns(guest):
            copy.wait_send()

    @pl.when(x_sender)
    def _():
        x_copy.wait_send()

    @pl.when(single)
    def _():
        c_copy.wait_send()
        for f in range(chunks):
            hand(0, f).wait_send()

    @pl.when(supplier)
    def _():
        for copy in supply():
            copy.wait_send()
        for copy in returns(0):
            copy.wait_recv()

    @pl.when(worker)
    def _():
        for copy in stores(own):
            copy.wait()


def layers(n_seq, n_pipe, section_inputs, cotangent, gain, w_gate, w_out, mix_first, mix_second):
    _, rows, width = section_inputs.shape
    block = rows // 2
    chunks = width // CHUNK
    span = n_seq * PIECE
    dma = pltpu.SemaphoreType.DMA
    wide = chunks * LANES
    out, g1, g2 = pl.pallas_call(
        functools.partial(kernel, n_seq, n_pipe),
        out_shape=(
            jax.ShapeDtypeStruct((rows, width), BF16),
            jax.ShapeDtypeStruct((2, block, block), F32),
            jax.ShapeDtypeStruct((2, block, block), F32),
        ),
        in_specs=[pl.BlockSpec(memory_space=pl.ANY)] * 7,
        out_specs=(pl.BlockSpec(memory_space=pl.ANY),) * 3,
        scratch_shapes=[
            pltpu.VMEM((2, rows, width), BF16),
            pltpu.VMEM((2, 1, width), F32),
            pltpu.VMEM((2, width, width), BF16),
            pltpu.VMEM((2, width, width), BF16),
            pltpu.VMEM((2, rows, block), BF16),
            pltpu.VMEM((2, rows, block), BF16),
            pltpu.VMEM((rows, width), BF16),
            pltpu.VMEM((2, rows, width), F32),
            pltpu.VMEM((2, rows, LANES), F32),
            pltpu.VMEM((rows, LANES), F32),
            pltpu.VMEM((rows, width), BF16),
            pltpu.VMEM((2, span, wide), BF16),
            pltpu.VMEM((span, span), BF16),
            pltpu.VMEM((span, span), BF16),
            pltpu.VMEM((2, span, span), BF16),
            pltpu.VMEM((2, span, span), BF16),
            pltpu.VMEM((span, span), BF16),
            pltpu.VMEM((span, span), BF16),
            pltpu.VMEM((2, span, wide), BF16),
            pltpu.VMEM((2, span, wide), BF16),
            pltpu.VMEM((2, span, wide), BF16),
            pltpu.VMEM((2, span, wide), BF16),
            pltpu.VMEM((2, rows, width), BF16),
            pltpu.VMEM((2, rows, width), F32),
            pltpu.VMEM((2, rows, width), F32),
            pltpu.VMEM((rows, width), F32),
            pltpu.VMEM((rows, width), BF16),
            pltpu.VMEM((rows, width), BF16),
            pltpu.VMEM((rows, width), F32),
            pltpu.VMEM((rows, width), F32),
            pltpu.VMEM((3, chunks, rows, CHUNK), BF16),
            pltpu.VMEM((8, rows), F32),
            pltpu.VMEM((8, rows), F32),
            pltpu.VMEM((2, rows, width), BF16),
            pltpu.VMEM((2, 2, block, block), F32),
            pltpu.VMEM((2, 2, block, block), F32),
            dma((6,)),
            dma((3,)),
            dma,
            dma,
            dma((2,)),
            dma((2,)),
            dma((2, chunks)),
            dma((2, chunks)),
            dma((chunks,)),
            dma((chunks,)),
            dma,
            dma,
            dma((2, 2)),
            dma((2, 2)),
            dma((2, 2)),
            dma((2, 2)),
            dma((2, 2)),
            dma((2, 2)),
            dma((2, 2)),
            dma((2, 2)),
            dma((4, 2, 2)),
            dma((2,)),
            dma((4,)),
            dma((4,)),
            dma((3,)),
            dma((3,)),
        ],
        compiler_params=pltpu.CompilerParams(
            collective_id=0, has_side_effects=True, vmem_limit_bytes=60 * 1024 * 1024
        ),
    )(
        section_inputs[0],
        cotangent,
        gain,
        w_gate[0],
        w_out[0],
        mix_first[0].reshape(rows, block),
        mix_second[0].reshape(rows, block),
    )
    return out[None], g1[None], g2[None]


def solution(mesh):
    placed = (
        P("pipe", "seq", None),
        P("seq", None),
        P("pipe", None),
        P("pipe", None, None),
        P("pipe", None, None),
        P("pipe", "seq", None, None),
        P("pipe", "seq", None, None),
    )
    return jax.shard_map(
        functools.partial(layers, mesh.shape["seq"], mesh.shape["pipe"]),
        mesh=mesh,
        in_specs=placed,
        out_specs=(
            P("pipe", "seq", None),
            P("pipe", "seq", None, None),
            P("pipe", "seq", None, None),
        ),
        check_vma=False,
    )
```

profile of v0, /device:TPU:1, one launch (start us, length us, event | category | flops | bytes accessed | tf_op | source)
XLA Modules:
  0.0 143.4 jit_solution(6745999924410618307)
XLA Ops:
  0.6 138.1 %shard_map.94 = (bf16[128,1536]{1,0:T(8,128)(2,1)}, f32[2,64,64]{2,1,0:T(8,128)}, f32[2,64,64]{2,1,0:T(8,128)}) custom-call(bf16[128,1536]{1,0:T(8,128)(2,1)} %bitcast.11, bf16[128,1536]{1,0:T(8,128)(2,1)} %cot_hbm.1, f32[1,1536]{1,0:T(1,128)} %gain_hbm.1, bf16[1536,1536]{1,0:T(8,128)(2,1)} %bitcast.8, bf16[1536,1536]{1,0:T(8,128)(2,1)} %bitcast.9, ...), custom_call_target="tpu_custom_call" | custom-call | tf_op jit(solution)/shard_map/pallas_call | solution.py:636
  138.7 1.8 %copy.13 = bf16[1,128,1536]{2,1,0:T(8,128)(2,1)} copy(bf16[1,128,1536]{2,1,0:T(8,128)(2,1)} %bitcast.10) | data formatting | bytes 786432
  140.5 1.5 %copy.14 = f32[1,2,64,64]{3,2,1,0:T(8,128)} copy(f32[1,2,64,64]{3,2,1,0:T(8,128)} %bitcast.13) | data formatting | bytes 65536
  141.9 1.5 %copy.15 = f32[1,2,64,64]{3,2,1,0:T(8,128)} copy(f32[1,2,64,64]{3,2,1,0:T(8,128)} %bitcast.12) | data formatting | bytes 65536
where the time goes:
time: 144 us; the launch traced here: 143 us
  Pallas kernels  138 us (96%)
  local copies, waits for them, and re-layouts  4.71 us (3%)
    pallas_call x1, Pallas kernels, layers(): pl.pallas_call(functools.partial(kernel, n_seq, n_pipe), out_shape=(jax.S...  138 us
    unnamed x3, local copies, waits for them, and re-layouts  4.71 us

commit v1 on v0

--- a/solution.py
+++ b/solution.py
@@ -15,6 +15,7 @@
 CHUNK = LANES * CUTS
 ROWS_TO = 4
 PIECE = ROWS_TO * CUTS
+PIECES = 4
 
 
 def iota(shape, axis):
@@ -71,10 +72,21 @@
     reader = jnp.where(plane == 2, 0, before)
     far = 8 if n_seq == 32 else 4
     bit_x, bit_y, bit_c = (me // far) % 2, (me // 2) % 2, me % 2
-    x_mate = me + far - 2 * far * bit_x
-    y_mate = me + 2 - 4 * bit_y
+    n_x, n_y = n_seq // far, far // 2
+    at_x, at_y = me // far, (me // 2) % n_y
+
+    def across(place, bit, count, j):
+        step = 1 - 2 * bit if j % 2 == 0 else 2 * bit - 1
+        return lax.rem(place + step + count, count)
+
+    def x_mate(j):
+        return me + far * (across(at_x, bit_x, n_x, j) - at_x)
+
+    def y_mate(j):
+        return me + 2 * (across(at_y, bit_y, n_y, j) - at_y)
+
     core_mate = me + 1 - 2 * bit_c
-    slab = width // 16
+    slab = width // (8 * PIECES)
 
     def seq_at(device):
         return {"seq": device}
@@ -250,12 +262,12 @@
 
     def slab_at(flip_x, flip_y, j):
         unit = 4 * (1 - bit_x if flip_x else bit_x) + 2 * (1 - bit_y if flip_y else bit_y) + bit_c
-        return pl.ds(pl.multiple_of((2 * unit + j) * slab, slab), slab)
+        return pl.ds(pl.multiple_of((PIECES * unit + j) * slab, slab), slab)
 
     def supply():
         given = []
         for i, (src, dst) in enumerate(((wg_hbm, r.wg), (wo_hbm, r.wo))):
-            for j in range(2):
+            for j in range(PIECES):
                 at = slab_at(0, 0, j)
                 given.append(
                     remote(
@@ -272,7 +284,7 @@
                 ((x_hbm, r.x), (m1_hbm, r.m1), (m2_hbm, r.m2), (gain_hbm, r.gain))
             )
         ]
-        return given + small[1:] + small[:1]
+        return small + given
 
     @pl.when(x_sender)
     def _():
@@ -292,8 +304,8 @@
     def pass_own(i, j):
         ref = piece(i, j)
         return (
-            remote(ref, ref, r.wxs_sem.at[i, j], r.wxr_sem.at[i, j], seq_at(x_mate)),
-            remote(ref, ref, r.wys_sem.at[i, j], r.wyr_sem.at[i, j], seq_at(y_mate)),
+            remote(ref, ref, r.wxs_sem.at[i, j], r.wxr_sem.at[i, j], seq_at(x_mate(j))),
+            remote(ref, ref, r.wys_sem.at[i, j], r.wyr_sem.at[i, j], seq_at(y_mate(j))),
             remote(ref, ref, r.wcs_sem.at[0, i, j], r.wc_sem.at[i], seq_at(core_mate)),
         )
 
@@ -304,7 +316,7 @@
 
     def pass_corner(i, j, flip_x, flip_y):
         ref = piece(i, j, flip_x, flip_y)
-        to = y_mate if flip_x else x_mate
+        to = y_mate(j) if flip_x else x_mate(j)
         return remote(ref, ref, r.wds_sem.at[i, j], r.wdr_sem.at[i, j], seq_at(to))
 
     def collect_own(i, j):
@@ -333,13 +345,12 @@
         pass_core(i, j, 1, 1).start()
 
     def collect_rest(i):
-        landed(weight(i).at[guest, : 8 * slab], r.wc_sem.at[i])
+        landed(weight(i).at[guest, : width // 2], r.wc_sem.at[i])
 
     def finish_guest():
-        for j in range(2):
+        for j in (PIECES - 2, PIECES - 1):
             collect_corner(1, j)
         collect_rest(1)
-        mixer(guest)
 
     @pl.when(worker)
     def _():
@@ -367,24 +378,23 @@
 
     @pl.when(double)
     def _():
-        collect_own(0, 0)
-        collect_own(0, 1)
-        collect_sides(0, 0)
-        collect_own(1, 0)
-        collect_sides(0, 1)
-        collect_own(1, 1)
-        collect_corner(0, 0)
-        collect_corner(0, 1)
-        collect_sides(1, 0)
-        for k, ref in ((1, r.m1), (2, r.m2), (3, r.gain)):
+        for k, ref in enumerate((r.x, r.m1, r.m2, r.gain)):
             landed(ref.at[guest], r.pr_sem.at[k])
         factors(guest)
-        collect_sides(1, 1)
-        landed(r.x.at[guest], r.pr_sem.at[0])
         norm(guest)
         forward(guest)
-        collect_rest(0)
-        gate(guest)
+        steps = [(i, j) for i in range(2) for j in range(PIECES)]
+        for t in range(len(steps) + 2):
+            if t < len(steps):
+                collect_own(*steps[t])
+            if t >= 2:
+                collect_sides(*steps[t - 2])
+            if 3 <= t < len(steps) + 1:
+                collect_corner(*steps[t - 3])
+            if t == PIECES + 2:
+                collect_rest(0)
+                gate(guest)
+                mixer(guest)
 
     @pl.when(double)
     def _():
@@ -593,7 +603,7 @@
         for f in range(chunks):
             sent(r.bsend.at[1], r.bs_sem.at[1, f], slice(f * LANES, (f + 1) * LANES))
         for i in range(2):
-            for j in range(2):
+            for j in range(PIECES):
                 for copy in pass_own(i, j):
                     copy.wait_send()
                 pass_core(i, j, 1, 0).wait_send()
@@ -691,15 +701,15 @@
             dma((chunks,)),
             dma,
             dma,
-            dma((2, 2)),
-            dma((2, 2)),
-            dma((2, 2)),
-            dma((2, 2)),
-            dma((2, 2)),
-            dma((2, 2)),
-            dma((2, 2)),
-            dma((2, 2)),
-            dma((4, 2, 2)),
+            dma((2, PIECES)),
+            dma((2, PIECES)),
+            dma((2, PIECES)),
+            dma((2, PIECES)),
+            dma((2, PIECES)),
+            dma((2, PIECES)),
+            dma((2, PIECES)),
+            dma((2, PIECES)),
+            dma((4, 2, PIECES)),
             dma((2,)),
             dma((4,)),
             dma((4,)),

time: 144 us -> 141 us (0.979)
  Pallas kernels: 138 us -> 135 us
    pallas_call x1, Pallas kernels: 138 us -> 135 us  [layers(): pl.pallas_call(functools.partial(kernel, n_seq, n_pipe), out_shape=(jax.S...]
where the time goes in v1:
time: 141 us; the launch traced here: 140 us
  Pallas kernels  135 us (96%)
  local copies, waits for them, and re-layouts  4.71 us (3%)
    pallas_call x1, Pallas kernels, layers(): pl.pallas_call(functools.partial(kernel, n_seq, n_pipe), out_shape=(jax.S...  135 us
    unnamed x3, local copies, waits for them, and re-layouts  4.71 us

profile of v1, /device:TPU:1, one launch (start us, length us, event | category | flops | bytes accessed | tf_op | source)
XLA Modules:
  0.0 140.1 jit_solution(8922075590073288606)
XLA Ops:
  0.6 134.8 %shard_map.94 = (bf16[128,1536]{1,0:T(8,128)(2,1)}, f32[2,64,64]{2,1,0:T(8,128)}, f32[2,64,64]{2,1,0:T(8,128)}) custom-call(bf16[128,1536]{1,0:T(8,128)(2,1)} %bitcast.11, bf16[128,1536]{1,0:T(8,128)(2,1)} %cot_hbm.1, f32[1,1536]{1,0:T(1,128)} %gain_hbm.1, bf16[1536,1536]{1,0:T(8,128)(2,1)} %bitcast.8, bf16[1536,1536]{1,0:T(8,128)(2,1)} %bitcast.9, ...), custom_call_target="tpu_custom_call" | custom-call | tf_op jit(solution)/shard_map/pallas_call | solution.py:646
  135.4 1.8 %copy.13 = bf16[1,128,1536]{2,1,0:T(8,128)(2,1)} copy(bf16[1,128,1536]{2,1,0:T(8,128)(2,1)} %bitcast.10) | data formatting | bytes 786432
  137.2 1.5 %copy.14 = f32[1,2,64,64]{3,2,1,0:T(8,128)} copy(f32[1,2,64,64]{3,2,1,0:T(8,128)} %bitcast.13) | data formatting | bytes 65536
  138.7 1.5 %copy.15 = f32[1,2,64,64]{3,2,1,0:T(8,128)} copy(f32[1,2,64,64]{3,2,1,0:T(8,128)} %bitcast.12) | data formatting | bytes 65536

commit v2 on v1

--- a/solution.py
+++ b/solution.py
@@ -150,13 +150,20 @@
             barrier, inc=1, device_id=pipe_at(lax.rem(plane + i, n_pipe)), device_id_type=MESH
         )
 
+    places_x = [lax.rem(at_x + d, n_x) for d in range(n_x)]
+    places_y = [lax.rem(at_y + d, n_y) for d in range(n_y)]
+    places_c = [bit_c, 1 - bit_c]
+    others = sorted(
+        ((dx, dy, dc) for dx in range(n_x) for dy in range(n_y) for dc in range(2) if dx or dy or dc),
+        key=lambda d: -3 * (min(d[0], n_x - d[0]) + min(d[1], n_y - d[1])) - d[2],
+    )
+
     def exchange(send, recv, send_sem, recv_sem, lanes):
         mine = pl.ds(pl.multiple_of(me * PIECE, PIECE), PIECE)
         pltpu.make_async_copy(send.at[mine, lanes], recv.at[mine, lanes], recv_sem).start()
 
-        @pl.loop(1, n_seq)
-        def _(i):
-            to = lax.rem(me + i, n_seq)
+        for dx, dy, dc in others:
+            to = far * places_x[dx] + 2 * places_y[dy] + places_c[dc]
             theirs = pl.ds(pl.multiple_of(to * PIECE, PIECE), PIECE)
             remote(send.at[theirs, lanes], recv.at[mine, lanes], send_sem, recv_sem, seq_at(to)).start()
 
@@ -200,10 +207,12 @@
         for c in range(CUTS):
             ref[c * rows : (c + 1) * rows, :] = jnp.where(cut_of_t == c, value, 0.0).astype(BF16)
 
+    def first_factor(at):
+        put_tall(r.dfwd, dot(sel1(), diagonal(r.m1[at])))
+
     def factors(at):
         d1 = diagonal(r.m1[at])
         d2 = diagonal(r.m2[at])
-        put_tall(r.dfwd, dot(sel1(), d1))
         put_tall(r.dbwd.at[at], dot(sel2(), d2, 1, 1))
         put_flat(r.efwd, dot(d2, sel2_t()))
         put_flat(r.ebwd.at[at], dot(d1, sel1_t(), 0, 0))
@@ -246,10 +255,7 @@
     @pl.when(worker)
     def _():
         loads[1].wait()
-        loads[2].wait()
-        put_flat(r.pick1, sel1_t().astype(F32))
-        put_flat(r.pick2, sel2_t().astype(F32))
-        factors(own)
+        first_factor(own)
         loads[0].wait()
         loads[3].wait()
         norm(own)
@@ -355,6 +361,10 @@
     @pl.when(worker)
     def _():
         forward(own)
+        loads[2].wait()
+        factors(own)
+        put_flat(r.pick1, sel1_t().astype(F32))
+        put_flat(r.pick2, sel2_t().astype(F32))
         loads[4].wait()
         gate(own)
         loads[5].wait()
@@ -380,6 +390,7 @@
     def _():
         for k, ref in enumerate((r.x, r.m1, r.m2, r.gain)):
             landed(ref.at[guest], r.pr_sem.at[k])
+        first_factor(guest)
         factors(guest)
         norm(guest)
         forward(guest)

time: 141 us -> 138 us (0.979)
  Pallas kernels: 135 us -> 132 us
    pallas_call x1, Pallas kernels: 135 us -> 132 us  [layers(): pl.pallas_call(functools.partial(kernel, n_seq, n_pipe), out_shape=(jax.S...]
where the time goes in v2:
time: 138 us; the launch traced here: 137 us
  Pallas kernels  132 us (96%)
  local copies, waits for them, and re-layouts  4.71 us (3%)
    pallas_call x1, Pallas kernels, layers(): pl.pallas_call(functools.partial(kernel, n_seq, n_pipe), out_shape=(jax.S...  132 us
    unnamed x3, local copies, waits for them, and re-layouts  4.71 us

profile of v2, /device:TPU:1, one launch (start us, length us, event | category | flops | bytes accessed | tf_op | source)
XLA Modules:
  0.0 137.2 jit_solution(9932900630684481539)
XLA Ops:
  0.6 131.8 %shard_map.94 = (bf16[128,1536]{1,0:T(8,128)(2,1)}, f32[2,64,64]{2,1,0:T(8,128)}, f32[2,64,64]{2,1,0:T(8,128)}) custom-call(bf16[128,1536]{1,0:T(8,128)(2,1)} %bitcast.11, bf16[128,1536]{1,0:T(8,128)(2,1)} %cot_hbm.1, f32[1,1536]{1,0:T(1,128)} %gain_hbm.1, bf16[1536,1536]{1,0:T(8,128)(2,1)} %bitcast.8, bf16[1536,1536]{1,0:T(8,128)(2,1)} %bitcast.9, ...), custom_call_target="tpu_custom_call" | custom-call | tf_op jit(solution)/shard_map/pallas_call | solution.py:657
  132.4 1.8 %copy.13 = bf16[1,128,1536]{2,1,0:T(8,128)(2,1)} copy(bf16[1,128,1536]{2,1,0:T(8,128)(2,1)} %bitcast.10) | data formatting | bytes 786432
  134.2 1.5 %copy.14 = f32[1,2,64,64]{3,2,1,0:T(8,128)} copy(f32[1,2,64,64]{3,2,1,0:T(8,128)} %bitcast.13) | data formatting | bytes 65536
  135.7 1.5 %copy.15 = f32[1,2,64,64]{3,2,1,0:T(8,128)} copy(f32[1,2,64,64]{3,2,1,0:T(8,128)} %bitcast.12) | data formatting | bytes 65536

commit v3 on v2

--- a/solution.py
+++ b/solution.py
@@ -458,10 +458,10 @@
                 r.anat[:, cols] - r.shift[...] * r.x[slot, :, cols].astype(F32)
             ).astype(BF16)
 
-    def stores(slot):
+    def stores(slot, kinds=range(3)):
+        pairs = ((r.res, out_hbm), (r.r1, g1_hbm), (r.r2, g2_hbm))
         return [
-            pltpu.make_async_copy(src.at[slot], dst, r.osem.at[k])
-            for k, (src, dst) in enumerate(((r.res, out_hbm), (r.r1, g1_hbm), (r.r2, g2_hbm)))
+            pltpu.make_async_copy(pairs[k][0].at[slot], pairs[k][1], r.osem.at[k]) for k in kinds
         ]
 
     def returns(slot, kinds=range(3)):
@@ -590,6 +590,11 @@
     @pl.when(double)
     def _():
         chain(1)
+
+        @pl.when(final)
+        def _():
+            stores(own, (0,))[0].start()
+
         results(1)
 
     @pl.when(double & jnp.logical_not(final))
@@ -600,9 +605,13 @@
         for copy in returns(1):
             copy.start()
 
+    @pl.when(worker & jnp.logical_not(final))
+    def _():
+        stores(own, (0,))[0].start()
+
     @pl.when(worker)
     def _():
-        for copy in stores(own):
+        for copy in stores(own, (1, 2)):
             copy.start()
         sent(r.fsend.at[own], r.fs_sem.at[own], whole)
         for f in range(chunks):

time: 138 us -> 138 us (level)
  no operation moved by 1% of the time
where the time goes in v3:
time: 138 us; the launch traced here: 137 us
  Pallas kernels  132 us (96%)
  local copies, waits for them, and re-layouts  4.71 us (3%)
    pallas_call x1, Pallas kernels, layers(): pl.pallas_call(functools.partial(kernel, n_seq, n_pipe), out_shape=(jax.S...  132 us
    unnamed x3, local copies, waits for them, and re-layouts  4.71 us

profile of v3, /device:TPU:1, one launch (start us, length us, event | category | flops | bytes accessed | tf_op | source)
XLA Modules:
  0.0 137.2 jit_solution(1471649649625227595)
XLA Ops:
  0.6 131.8 %shard_map.94 = (bf16[128,1536]{1,0:T(8,128)(2,1)}, f32[2,64,64]{2,1,0:T(8,128)}, f32[2,64,64]{2,1,0:T(8,128)}) custom-call(bf16[128,1536]{1,0:T(8,128)(2,1)} %bitcast.11, bf16[128,1536]{1,0:T(8,128)(2,1)} %cot_hbm.1, f32[1,1536]{1,0:T(1,128)} %gain_hbm.1, bf16[1536,1536]{1,0:T(8,128)(2,1)} %bitcast.8, bf16[1536,1536]{1,0:T(8,128)(2,1)} %bitcast.9, ...), custom_call_target="tpu_custom_call" | custom-call | tf_op jit(solution)/shard_map/pallas_call | solution.py:666
  132.4 1.8 %copy.13 = bf16[1,128,1536]{2,1,0:T(8,128)(2,1)} copy(bf16[1,128,1536]{2,1,0:T(8,128)(2,1)} %bitcast.10) | data formatting | bytes 786432
  134.2 1.5 %copy.14 = f32[1,2,64,64]{3,2,1,0:T(8,128)} copy(f32[1,2,64,64]{3,2,1,0:T(8,128)} %bitcast.13) | data formatting | bytes 65536
  135.7 1.5 %copy.15 = f32[1,2,64,64]{3,2,1,0:T(8,128)} copy(f32[1,2,64,64]{3,2,1,0:T(8,128)} %bitcast.12) | data formatting | bytes 65536
